TPU v7x, 32 devices: a whole 2x2x4 slice. The times are simulated.
32 devices in a mesh: blade: 1, prow: 4 (over x, core), pcol: 8 (over z, y).
Axes of the slice: x: 2, y: 2, z: 4, core: 2. Of those that a mesh axis runs over, the one named last changes fastest.
Arguments:
- factor: float32 [4, 4, 512, 4, 8, 256], P('blade', 'prow', None, None, 'pcol'), may hold values from -0.03125 to 0.03125
- inverses: float32 [4, 8, 256, 4, 512], P('blade', 'pcol', None, 'prow'), as said below
- targets: float32 [8, 3, 8192], P('blade'), may hold values from -6 to 6
- anchors: float32 [3, 8192], P('blade'), may hold values from 0 to 1, as said below
- nodes: float32 [3, 16, 128, 128], P('blade', 'prow', 'pcol'), as said below
Outputs:
- coefficients: float32 [8, 3, 8192], P('blade')
- moved: float32 [8, 3, 16, 128, 128], P('blade', None, 'prow', 'pcol')
- jacobian: float32 [8, 16, 128, 128], P('blade', 'prow', 'pcol')
Inputs may be any that keep to these rules, and one draw needn't show every extreme that they name: `inverses`: 4 blocks of 2048 x 2048 real entries. `anchors`: positions in the unit cube. `nodes`: positions inside a box around the unit cube, ordered along span, chord and normal.
All inputs are finite; a program needn't handle non-finite values.
Results may differ from a plain program's by a relative error of at most 0.0003.
Values sent between devices are 32-bit elements; how exact they have to be, the bound alone decides.
A program may use at most 64 MiB of HBM per device.

v0:
```python
import math

import jax
import jax.numpy as jnp
from jax import lax
from jax.sharding import PartitionSpec as P

support_radius = 0.1
highest = lax.Precision.HIGHEST


def padded_2(cells, sides, width):
    for axis, dim in sides:
        count = lax.axis_size(axis)
        ends = count - 1
        head = lax.slice_in_dim(cells, 0, width, axis=dim)
        tail = lax.slice_in_dim(cells, cells.shape[dim] - width, cells.shape[dim], axis=dim)
        cells = jnp.concatenate(
            [
                lax.ppermute(tail, axis, [(i, (i + 1) % count) for i in range(ends)]),
                cells,
                lax.ppermute(head, axis, [((i + 1) % count, i) for i in range(ends)]),
            ],
            axis=dim,
        )
    return cells


def wendland(dist_sq):
    scaled_dist = jnp.sqrt(dist_sq) / support_radius
    falloff = jnp.maximum(1.0 - scaled_dist, 0.0)
    return falloff**4 * (4.0 * scaled_dist + 1.0)


def extend(values, axis_pos):
    extent = values.shape[axis_pos]
    low_layer = 2.0 * lax.slice_in_dim(values, 0, 1, axis=axis_pos) - lax.slice_in_dim(
        values, 1, 2, axis=axis_pos
    )
    high_layer = 2.0 * lax.slice_in_dim(
        values, extent - 1, extent, axis=axis_pos
    ) - lax.slice_in_dim(values, extent - 2, extent - 1, axis=axis_pos)
    return jnp.concatenate([low_layer, values, high_layer], axis=axis_pos)


def close_edges(padded, axis_pos, at_low, at_high):
    extent = padded.shape[axis_pos]
    low_layer = 2.0 * lax.slice_in_dim(padded, 1, 2, axis=axis_pos) - lax.slice_in_dim(
        padded, 2, 3, axis=axis_pos
    )
    high_layer = 2.0 * lax.slice_in_dim(
        padded, extent - 2, extent - 1, axis=axis_pos
    ) - lax.slice_in_dim(padded, extent - 3, extent - 2, axis=axis_pos)
    first_layer = jnp.where(at_low, low_layer, lax.slice_in_dim(padded, 0, 1, axis=axis_pos))
    last_layer = jnp.where(
        at_high, high_layer, lax.slice_in_dim(padded, extent - 1, extent, axis=axis_pos)
    )
    inner_layers = lax.slice_in_dim(padded, 1, extent - 1, axis=axis_pos)
    return jnp.concatenate([first_layer, inner_layers, last_layer], axis=axis_pos)


def jacobian_of(extended, scales):
    d_span = (extended[:, :, 2:, 1:-1, 1:-1] - extended[:, :, :-2, 1:-1, 1:-1]) * scales[0]
    d_chord = (extended[:, :, 1:-1, 2:, 1:-1] - extended[:, :, 1:-1, :-2, 1:-1]) * scales[1]
    d_normal = (extended[:, :, 1:-1, 1:-1, 2:] - extended[:, :, 1:-1, 1:-1, :-2]) * scales[2]
    cross_first = d_chord[:, 1] * d_normal[:, 2] - d_chord[:, 2] * d_normal[:, 1]
    cross_second = d_chord[:, 2] * d_normal[:, 0] - d_chord[:, 0] * d_normal[:, 2]
    cross_third = d_chord[:, 0] * d_normal[:, 1] - d_chord[:, 1] * d_normal[:, 0]
    return d_span[:, 0] * cross_first + d_span[:, 1] * cross_second + d_span[:, 2] * cross_third


def shards(factor, inverses, targets, anchors, nodes):
    row_devs = lax.axis_size("prow")
    col_devs = lax.axis_size("pcol")
    prow_id = lax.axis_index("prow")
    pcol_id = lax.axis_index("pcol")
    local_factor = factor[:, 0, :, :, 0, :]
    local_inverses = inverses[:, 0, :, 0, :]
    block_total = local_factor.shape[0]
    row_piece = local_factor.shape[1]
    col_piece = local_factor.shape[3]
    block_len = row_piece * row_devs
    instances = targets.shape[0]
    row_count = instances * targets.shape[1]
    point_total = targets.shape[2]
    right_sides = targets.reshape(row_count, block_total, block_len)
    forward = jnp.zeros((row_count, block_total, col_piece), jnp.float32)
    for block_id in range(block_total):
        partial_value = jnp.einsum(
            "rjc,wjc->wr", local_factor[block_id], forward, precision=highest
        )
        own_rows = lax.dynamic_slice_in_dim(
            right_sides[:, block_id], prow_id * row_piece, row_piece, 1
        )
        summed = lax.psum(partial_value, "pcol")
        term = jnp.einsum(
            "ab,wb->wa", local_inverses[block_id], own_rows - summed, precision=highest
        )
        solved = lax.psum(term, "prow")
        forward = forward.at[:, block_id].set(solved)
    coeffs = jnp.zeros((row_count, block_total, row_piece), jnp.float32)
    for block_id in reversed(range(block_total)):
        col_blocks = local_factor[:, :, block_id]
        forward_block = forward[:, block_id]
        partial_value = jnp.einsum("jrc,wjr->wc", col_blocks, coeffs, precision=highest)
        summed = lax.psum(partial_value, "prow")
        term = jnp.einsum(
            "ab,wa->wb", local_inverses[block_id], forward_block - summed, precision=highest
        )
        solved = lax.psum(term, "pcol")
        coeffs = coeffs.at[:, block_id].set(solved)
    coeffs = lax.all_gather(coeffs, "prow", axis=2, tiled=True)
    coef_matrix = coeffs.reshape(row_count, point_total)
    flat = nodes.reshape(3, -1)
    node_count = flat.shape[1]
    block_size = min(512, node_count)
    node_groups = flat.reshape(3, node_count // block_size, block_size).transpose(1, 0, 2)

    def deform(node_group):
        dist_sq = (node_group[0][:, None] - anchors[0][None, :]) ** 2
        dist_sq = dist_sq + (node_group[1][:, None] - anchors[1][None, :]) ** 2
        dist_sq = dist_sq + (node_group[2][:, None] - anchors[2][None, :]) ** 2
        return lax.dot_general(
            coef_matrix, wendland(dist_sq), (((1,), (1,)), ((), ())), precision=highest
        )

    shifts = lax.map(deform, node_groups)
    shifts = shifts.transpose(1, 0, 2).reshape((instances,) + nodes.shape)
    moved = nodes[None] + 2.0 / math.sqrt(point_total) * shifts
    padded = padded_2(moved, (("prow", 2), ("pcol", 3)), 1)
    padded = close_edges(padded, 2, prow_id == 0, prow_id == row_devs - 1)
    padded = close_edges(padded, 3, pcol_id == 0, pcol_id == col_devs - 1)
    extended = extend(padded, 4)
    scales = (
        nodes.shape[1] * row_devs / 2.0,
        nodes.shape[2] * col_devs / 2.0,
        nodes.shape[3] / 2.0,
    )
    jacobian = jacobian_of(extended, scales)
    return (coeffs.reshape(instances, 3, point_total), moved, jacobian)


def solution(mesh):
    placed = (
        P("blade", "prow", None, None, "pcol", None),
        P("blade", "pcol", None, "prow", None),
        P("blade", None, None),
        P("blade", None),
        P("blade", "prow", "pcol", None),
    )
    return jax.shard_map(
        shards,
        mesh=mesh,
        in_specs=placed,
        out_specs=(
            P("blade", None, None),
            P("blade", None, "prow", "pcol", None),
            P("blade", "prow", "pcol", None),
        ),
        check_vma=False,
    )
```

profile of v0, /device:TPU:1, one launch (start us, length us, event | category | flops | bytes accessed | tf_op | source)
XLA Modules:
  0.0 1282.0 jit_solution(8106645865025207151)
XLA Ops:
  31.5 32.1 %psum.112 = f32[24,512]{1,0:T(8,128)S(1)} all-reduce(f32[24,512]{1,0:T(8,128)} %fusion.58), channel_id=1, replica_groups=mesh['blade'=1,'prow'=4,'pcol'=8] {'pcol'}, use_global_device_ids=true, to_apply=%region_0.0 | all-reduce | flops 12288 | bytes 98304 | tf_op jit(solution)/shard_map/psum | solution.py:95
  90.3 27.0 %psum.114 = f32[24,512]{1,0:T(8,128)S(1)} all-reduce(f32[24,512]{1,0:T(8,128)} %fusion.61), channel_id=1, replica_groups=mesh['blade'=1,'prow'=4,'pcol'=8] {'pcol'}, use_global_device_ids=true, to_apply=%region_2.0 | all-reduce | flops 12288 | bytes 98304 | tf_op jit(solution)/shard_map/psum | solution.py:95
  141.6 28.3 %psum.116 = f32[24,512]{1,0:T(8,128)S(1)} all-reduce(f32[24,512]{1,0:T(8,128)S(1)} %fusion.64), channel_id=1, replica_groups=mesh['blade'=1,'prow'=4,'pcol'=8] {'pcol'}, use_global_device_ids=true, to_apply=%region_4.0 | all-reduce | flops 12288 | bytes 98304 | tf_op jit(solution)/shard_map/psum | solution.py:95
  196.0 27.0 %psum.118 = f32[24,512]{1,0:T(8,128)S(1)} all-reduce(f32[24,512]{1,0:T(8,128)} %fusion.67), channel_id=1, replica_groups=mesh['blade'=1,'prow'=4,'pcol'=8] {'pcol'}, use_global_device_ids=true, to_apply=%region_6.0 | all-reduce | flops 12288 | bytes 98304 | tf_op jit(solution)/shard_map/psum | solution.py:95
  263.5 28.2 %psum.121 = f32[24,1,512]{2,0,1:T(8,128)S(1)} all-reduce(f32[24,1,512]{2,0,1:T(8,128)S(1)} %convolution_bitcast_fusion.3), channel_id=1, replica_groups=mesh['blade'=1,'prow'=4,'pcol'=8] {'pcol'}, use_global_device_ids=true, to_apply=%region_9.0 | all-reduce | flops 12288 | bytes 98304 | tf_op jit(solution)/shard_map/psum | solution.py:110
  313.8 26.5 %psum.123 = f32[24,1,512]{2,0,1:T(8,128)S(1)} all-reduce(f32[24,1,512]{2,0,1:T(8,128)S(1)} %convolution_bitcast_fusion.2), channel_id=1, replica_groups=mesh['blade'=1,'prow'=4,'pcol'=8] {'pcol'}, use_global_device_ids=true, to_apply=%region_11.0 | all-reduce | flops 12288 | bytes 98304 | tf_op jit(solution)/shard_map/psum | solution.py:110
  360.4 28.2 %psum.125 = f32[24,1,512]{2,0,1:T(8,128)S(1)} all-reduce(f32[24,1,512]{2,0,1:T(8,128)S(1)} %convolution_bitcast_fusion.1), channel_id=1, replica_groups=mesh['blade'=1,'prow'=4,'pcol'=8] {'pcol'}, use_global_device_ids=true, to_apply=%region_13.0 | all-reduce | flops 12288 | bytes 98304 | tf_op jit(solution)/shard_map/psum | solution.py:110
  450.1 808.1 %while.20 = (s32[]{:T(128)}, f32[16,24,512]{2,1,0:T(8,128)S(1)}, f32[16,3,512]{2,0,1:T(8,128)S(1)}, f32[3,8192]{1,0:T(4,128)S(1)}, f32[24,8192]{1,0:T(8,128)S(1)}, /*index=5*/s32[]{:T(128)}, s32[]{:T(128)}, s32[]{}, s32[]{}) while((s32[]{:T(128)}, f32[16,24,512]{2,1,0:T(8,128)S(1)}, f32[16,3,512]{2,0,1:T(8,128)S(1)}, ...), condition=%wide.region_17.0_spmd, body=%wide.region_16.0_spmd.sunk | while | flops 1275068416 | bytes 1149061 | solution.py:127
  450.2 50.4 %fusion.144 = f32[16,24,512]{2,1,0:T(8,128)S(1)} fusion(f32[16,24,512]{2,1,0:T(8,128)S(1)} %get-tuple-element.271, s32[]{:T(128)} %get-tuple-element.270, f32[24,8192]{1,0:T(8,128)S(1)} %get-tuple-element.283, f32[8192]{0:T(1024)S(1)} %bitcast.168, f32[512]{0:T(512)S(1)} %bitcast.174, f32[8192]{0:T(1024)S(1)} %bitcast.169, f32[512]{0:T(512)S(1)} %bitcast.173, ...), kind=kOutput, calls=%fused_computation.29.clone.1 | convolution fusion | flops 1275068416 | bytes 940036 | tf_op jit(solution)/shard_map/while/body/eval_jaxpr/dot_general | solution.py:123
  500.7 50.4 %fusion.144 = f32[16,24,512]{2,1,0:T(8,128)S(1)} fusion(f32[16,24,512]{2,1,0:T(8,128)S(1)} %get-tuple-element.271, s32[]{:T(128)} %get-tuple-element.270, f32[24,8192]{1,0:T(8,128)S(1)} %get-tuple-element.283, f32[8192]{0:T(1024)S(1)} %bitcast.168, f32[512]{0:T(512)S(1)} %bitcast.174, f32[8192]{0:T(1024)S(1)} %bitcast.169, f32[512]{0:T(512)S(1)} %bitcast.173, ...), kind=kOutput, calls=%fused_computation.29.clone.1 | convolution fusion | flops 1275068416 | bytes 940036 | tf_op jit(solution)/shard_map/while/body/eval_jaxpr/dot_general | solution.py:123
  551.2 50.4 %fusion.144 = f32[16,24,512]{2,1,0:T(8,128)S(1)} fusion(f32[16,24,512]{2,1,0:T(8,128)S(1)} %get-tuple-element.271, s32[]{:T(128)} %get-tuple-element.270, f32[24,8192]{1,0:T(8,128)S(1)} %get-tuple-element.283, f32[8192]{0:T(1024)S(1)} %bitcast.168, f32[512]{0:T(512)S(1)} %bitcast.174, f32[8192]{0:T(1024)S(1)} %bitcast.169, f32[512]{0:T(512)S(1)} %bitcast.173, ...), kind=kOutput, calls=%fused_computation.29.clone.1 | convolution fusion | flops 1275068416 | bytes 940036 | tf_op jit(solution)/shard_map/while/body/eval_jaxpr/dot_general | solution.py:123
  601.7 50.4 %fusion.144 = f32[16,24,512]{2,1,0:T(8,128)S(1)} fusion(f32[16,24,512]{2,1,0:T(8,128)S(1)} %get-tuple-element.271, s32[]{:T(128)} %get-tuple-element.270, f32[24,8192]{1,0:T(8,128)S(1)} %get-tuple-element.283, f32[8192]{0:T(1024)S(1)} %bitcast.168, f32[512]{0:T(512)S(1)} %bitcast.174, f32[8192]{0:T(1024)S(1)} %bitcast.169, f32[512]{0:T(512)S(1)} %bitcast.173, ...), kind=kOutput, calls=%fused_computation.29.clone.1 | convolution fusion | flops 1275068416 | bytes 940036 | tf_op jit(solution)/shard_map/while/body/eval_jaxpr/dot_general | solution.py:123
  652.2 50.4 %fusion.144 = f32[16,24,512]{2,1,0:T(8,128)S(1)} fusion(f32[16,24,512]{2,1,0:T(8,128)S(1)} %get-tuple-element.271, s32[]{:T(128)} %get-tuple-element.270, f32[24,8192]{1,0:T(8,128)S(1)} %get-tuple-element.283, f32[8192]{0:T(1024)S(1)} %bitcast.168, f32[512]{0:T(512)S(1)} %bitcast.174, f32[8192]{0:T(1024)S(1)} %bitcast.169, f32[512]{0:T(512)S(1)} %bitcast.173, ...), kind=kOutput, calls=%fused_computation.29.clone.1 | convolution fusion | flops 1275068416 | bytes 940036 | tf_op jit(solution)/shard_map/while/body/eval_jaxpr/dot_general | solution.py:123
  702.7 50.4 %fusion.144 = f32[16,24,512]{2,1,0:T(8,128)S(1)} fusion(f32[16,24,512]{2,1,0:T(8,128)S(1)} %get-tuple-element.271, s32[]{:T(128)} %get-tuple-element.270, f32[24,8192]{1,0:T(8,128)S(1)} %get-tuple-element.283, f32[8192]{0:T(1024)S(1)} %bitcast.168, f32[512]{0:T(512)S(1)} %bitcast.174, f32[8192]{0:T(1024)S(1)} %bitcast.169, f32[512]{0:T(512)S(1)} %bitcast.173, ...), kind=kOutput, calls=%fused_computation.29.clone.1 | convolution fusion | flops 1275068416 | bytes 940036 | tf_op jit(solution)/shard_map/while/body/eval_jaxpr/dot_general | solution.py:123
  753.3 50.4 %fusion.144 = f32[16,24,512]{2,1,0:T(8,128)S(1)} fusion(f32[16,24,512]{2,1,0:T(8,128)S(1)} %get-tuple-element.271, s32[]{:T(128)} %get-tuple-element.270, f32[24,8192]{1,0:T(8,128)S(1)} %get-tuple-element.283, f32[8192]{0:T(1024)S(1)} %bitcast.168, f32[512]{0:T(512)S(1)} %bitcast.174, f32[8192]{0:T(1024)S(1)} %bitcast.169, f32[512]{0:T(512)S(1)} %bitcast.173, ...), kind=kOutput, calls=%fused_computation.29.clone.1 | convolution fusion | flops 1275068416 | bytes 940036 | tf_op jit(solution)/shard_map/while/body/eval_jaxpr/dot_general | solution.py:123
  803.8 50.4 %fusion.144 = f32[16,24,512]{2,1,0:T(8,128)S(1)} fusion(f32[16,24,512]{2,1,0:T(8,128)S(1)} %get-tuple-element.271, s32[]{:T(128)} %get-tuple-element.270, f32[24,8192]{1,0:T(8,128)S(1)} %get-tuple-element.283, f32[8192]{0:T(1024)S(1)} %bitcast.168, f32[512]{0:T(512)S(1)} %bitcast.174, f32[8192]{0:T(1024)S(1)} %bitcast.169, f32[512]{0:T(512)S(1)} %bitcast.173, ...), kind=kOutput, calls=%fused_computation.29.clone.1 | convolution fusion | flops 1275068416 | bytes 940036 | tf_op jit(solution)/shard_map/while/body/eval_jaxpr/dot_general | solution.py:123
  854.3 50.4 %fusion.144 = f32[16,24,512]{2,1,0:T(8,128)S(1)} fusion(f32[16,24,512]{2,1,0:T(8,128)S(1)} %get-tuple-element.271, s32[]{:T(128)} %get-tuple-element.270, f32[24,8192]{1,0:T(8,128)S(1)} %get-tuple-element.283, f32[8192]{0:T(1024)S(1)} %bitcast.168, f32[512]{0:T(512)S(1)} %bitcast.174, f32[8192]{0:T(1024)S(1)} %bitcast.169, f32[512]{0:T(512)S(1)} %bitcast.173, ...), kind=kOutput, calls=%fused_computation.29.clone.1 | convolution fusion | flops 1275068416 | bytes 940036 | tf_op jit(solution)/shard_map/while/body/eval_jaxpr/dot_general | solution.py:123
  904.8 50.4 %fusion.144 = f32[16,24,512]{2,1,0:T(8,128)S(1)} fusion(f32[16,24,512]{2,1,0:T(8,128)S(1)} %get-tuple-element.271, s32[]{:T(128)} %get-tuple-element.270, f32[24,8192]{1,0:T(8,128)S(1)} %get-tuple-element.283, f32[8192]{0:T(1024)S(1)} %bitcast.168, f32[512]{0:T(512)S(1)} %bitcast.174, f32[8192]{0:T(1024)S(1)} %bitcast.169, f32[512]{0:T(512)S(1)} %bitcast.173, ...), kind=kOutput, calls=%fused_computation.29.clone.1 | convolution fusion | flops 1275068416 | bytes 940036 | tf_op jit(solution)/shard_map/while/body/eval_jaxpr/dot_general | solution.py:123
  955.3 50.4 %fusion.144 = f32[16,24,512]{2,1,0:T(8,128)S(1)} fusion(f32[16,24,512]{2,1,0:T(8,128)S(1)} %get-tuple-element.271, s32[]{:T(128)} %get-tuple-element.270, f32[24,8192]{1,0:T(8,128)S(1)} %get-tuple-element.283, f32[8192]{0:T(1024)S(1)} %bitcast.168, f32[512]{0:T(512)S(1)} %bitcast.174, f32[8192]{0:T(1024)S(1)} %bitcast.169, f32[512]{0:T(512)S(1)} %bitcast.173, ...), kind=kOutput, calls=%fused_computation.29.clone.1 | convolution fusion | flops 1275068416 | bytes 940036 | tf_op jit(solution)/shard_map/while/body/eval_jaxpr/dot_general | solution.py:123
  1005.8 50.4 %fusion.144 = f32[16,24,512]{2,1,0:T(8,128)S(1)} fusion(f32[16,24,512]{2,1,0:T(8,128)S(1)} %get-tuple-element.271, s32[]{:T(128)} %get-tuple-element.270, f32[24,8192]{1,0:T(8,128)S(1)} %get-tuple-element.283, f32[8192]{0:T(1024)S(1)} %bitcast.168, f32[512]{0:T(512)S(1)} %bitcast.174, f32[8192]{0:T(1024)S(1)} %bitcast.169, f32[512]{0:T(512)S(1)} %bitcast.173, ...), kind=kOutput, calls=%fused_computation.29.clone.1 | convolution fusion | flops 1275068416 | bytes 940036 | tf_op jit(solution)/shard_map/while/body/eval_jaxpr/dot_general | solution.py:123
  1056.3 50.4 %fusion.144 = f32[16,24,512]{2,1,0:T(8,128)S(1)} fusion(f32[16,24,512]{2,1,0:T(8,128)S(1)} %get-tuple-element.271, s32[]{:T(128)} %get-tuple-element.270, f32[24,8192]{1,0:T(8,128)S(1)} %get-tuple-element.283, f32[8192]{0:T(1024)S(1)} %bitcast.168, f32[512]{0:T(512)S(1)} %bitcast.174, f32[8192]{0:T(1024)S(1)} %bitcast.169, f32[512]{0:T(512)S(1)} %bitcast.173, ...), kind=kOutput, calls=%fused_computation.29.clone.1 | convolution fusion | flops 1275068416 | bytes 940036 | tf_op jit(solution)/shard_map/while/body/eval_jaxpr/dot_general | solution.py:123
  1106.8 50.4 %fusion.144 = f32[16,24,512]{2,1,0:T(8,128)S(1)} fusion(f32[16,24,512]{2,1,0:T(8,128)S(1)} %get-tuple-element.271, s32[]{:T(128)} %get-tuple-element.270, f32[24,8192]{1,0:T(8,128)S(1)} %get-tuple-element.283, f32[8192]{0:T(1024)S(1)} %bitcast.168, f32[512]{0:T(512)S(1)} %bitcast.174, f32[8192]{0:T(1024)S(1)} %bitcast.169, f32[512]{0:T(512)S(1)} %bitcast.173, ...), kind=kOutput, calls=%fused_computation.29.clone.1 | convolution fusion | flops 1275068416 | bytes 940036 | tf_op jit(solution)/shard_map/while/body/eval_jaxpr/dot_general | solution.py:123
  1157.3 50.4 %fusion.144 = f32[16,24,512]{2,1,0:T(8,128)S(1)} fusion(f32[16,24,512]{2,1,0:T(8,128)S(1)} %get-tuple-element.271, s32[]{:T(128)} %get-tuple-element.270, f32[24,8192]{1,0:T(8,128)S(1)} %get-tuple-element.283, f32[8192]{0:T(1024)S(1)} %bitcast.168, f32[512]{0:T(512)S(1)} %bitcast.174, f32[8192]{0:T(1024)S(1)} %bitcast.169, f32[512]{0:T(512)S(1)} %bitcast.173, ...), kind=kOutput, calls=%fused_computation.29.clone.1 | convolution fusion | flops 1275068416 | bytes 940036 | tf_op jit(solution)/shard_map/while/body/eval_jaxpr/dot_general | solution.py:123
  1207.8 50.4 %fusion.144 = f32[16,24,512]{2,1,0:T(8,128)S(1)} fusion(f32[16,24,512]{2,1,0:T(8,128)S(1)} %get-tuple-element.271, s32[]{:T(128)} %get-tuple-element.270, f32[24,8192]{1,0:T(8,128)S(1)} %get-tuple-element.283, f32[8192]{0:T(1024)S(1)} %bitcast.168, f32[512]{0:T(512)S(1)} %bitcast.174, f32[8192]{0:T(1024)S(1)} %bitcast.169, f32[512]{0:T(512)S(1)} %bitcast.173, ...), kind=kOutput, calls=%fused_computation.29.clone.1 | convolution fusion | flops 1275068416 | bytes 940036 | tf_op jit(solution)/shard_map/while/body/eval_jaxpr/dot_general | solution.py:123
  (129 shorter events, 276.9 us)
Async XLA Ops:
  9.9 8.8 copy-start.5
  243.1 1.0 copy-start
  389.5 60.5 %copy-start.3 = (f32[3,4,16,128]{3,2,1,0:T(8,128)S(1)}, f32[3,4,16,128]{3,2,1,0:T(8,128)}, u32[]{:S(2)}) copy-start(f32[3,4,16,128]{3,2,1,0:T(8,128)} %param.27) | copy-start | bytes 294916
  389.5 60.5 %copy-start.1 = (f32[3,8192]{1,0:T(4,128)S(1)}, f32[3,8192]{1,0:T(4,128)}, u32[]{:S(2)}) copy-start(f32[3,8192]{1,0:T(4,128)} %param.26) | copy-start | bytes 294916
  389.6 60.5 %copy-start.6 = (f32[16,24,512]{2,1,0:T(8,128)S(1)}, f32[16,24,512]{2,1,0:T(8,128)}, u32[]{:S(2)}) copy-start(f32[16,24,512]{2,1,0:T(8,128)} %custom-call.1) | copy-start | bytes 2359300
  1258.8 4.7 copy-start.4
  1258.9 9.8 copy-start.2
  1259.0 4.6 collective-permute-start
  1261.0 7.0 collective-permute-start.1
  1268.8 5.8 collective-permute-start.2
  1270.7 5.4 collective-permute-start.3
where the time goes:
time: 1280 us
  matrix products  827 us (65%)
  blocking collectives  363 us (28%)
  local copies, waits for them, and re-layouts  71.1 us (6%)
    dot_general x16, matrix products, deform(): lax.dot_general(coef_matrix, wendland(dist_sq), (((1,), (1,)), ((), ())),...  806 us
    psum x4, blocking collectives, shards(): summed = lax.psum(partial_value, 'pcol')  114 us
    psum x4, blocking collectives, shards(): solved = lax.psum(term, 'pcol')  109 us
    psum x4, blocking collectives, shards(): solved = lax.psum(term, 'prow')  70.5 us
    psum x3, blocking collectives, shards(): summed = lax.psum(partial_value, 'prow')  52.8 us
  transfers between devices with their start and end apart: 4, of which 3 were waited for; matrix products, arithmetic and copies ran while one was open for 0% of the time, Pallas kernels for 0%

commit v1 on v0

v1 whole, which is shorter than its diff:
```python
import functools
import math

import jax
import jax.numpy as jnp
from jax import lax
from jax.experimental import pallas as pl
from jax.experimental.pallas import tpu as pltpu
from jax.sharding import PartitionSpec as P

support_radius = 0.1
reach = support_radius + 1e-4
BLOCK = 128
CHUNK = 256
highest = lax.Precision.HIGHEST


def deform_kernel(order_ref, bounds_ref, stacked_ref, nodes_ref, out_ref, table, gathered, coefs, sums):
    rows = sums.shape[0]
    groups = nodes_ref.shape[0]
    width = nodes_ref.shape[2]
    blocks = table.shape[0] // BLOCK

    @pl.loop(0, blocks)
    def _(b):
        start = pl.multiple_of(b * BLOCK, BLOCK)
        piece = stacked_ref[:, pl.ds(start, BLOCK)]
        padding = jnp.zeros((BLOCK - piece.shape[0], BLOCK), jnp.float32)
        table[pl.ds(start, BLOCK), :] = jnp.concatenate([piece, padding], axis=0).T

    @pl.loop(bounds_ref[2 * groups], bounds_ref[2 * groups + 1])
    def _(b):
        start = pl.multiple_of(b * BLOCK, BLOCK)

        @pl.loop(0, BLOCK // 16)
        def _(i):
            base = start + i * 16
            for j in range(16):
                gathered[pl.ds(base + j, 1), :] = table[pl.ds(order_ref[base + j], 1), :]

        turned = gathered[pl.ds(start, BLOCK), :].T
        exact = turned[:rows]
        high = exact.astype(jnp.bfloat16)
        low = (exact - high.astype(jnp.float32)).astype(jnp.bfloat16)
        coefs[b, 0] = jnp.concatenate([high, low], axis=0)

    for g in range(groups):
        sums[...] = jnp.zeros_like(sums)

        @pl.loop(bounds_ref[2 * g], bounds_ref[2 * g + 1])
        def _(b):
            start = pl.multiple_of(b * BLOCK, BLOCK)
            places = gathered[pl.ds(start, BLOCK), :]
            px = jnp.broadcast_to(places[:, rows : rows + 1], (BLOCK, CHUNK))
            py = jnp.broadcast_to(places[:, rows + 1 : rows + 2], (BLOCK, CHUNK))
            pz = jnp.broadcast_to(places[:, rows + 2 : rows + 3], (BLOCK, CHUNK))
            both = coefs[b, 0]
            for c in range(width // CHUNK):
                cut = slice(c * CHUNK, (c + 1) * CHUNK)
                dx = nodes_ref[g, 0:1, cut] - px
                dy = nodes_ref[g, 1:2, cut] - py
                dz = nodes_ref[g, 2:3, cut] - pz
                dist_sq = dx * dx + dy * dy + dz * dz
                dist = dist_sq * lax.rsqrt(jnp.maximum(dist_sq, 1e-30))
                falloff = jnp.maximum(1.0 - dist * (1.0 / support_radius), 0.0)
                square = falloff * falloff
                phi = square * square * (5.0 - 4.0 * falloff)
                phi_high = phi.astype(jnp.bfloat16)
                phi_low = (phi - phi_high.astype(jnp.float32)).astype(jnp.bfloat16)
                first = jnp.dot(both, phi_high, preferred_element_type=jnp.float32)
                second = jnp.dot(both, phi_low, preferred_element_type=jnp.float32)
                sums[:, cut] += first[:rows] + first[rows:] + second[:rows]

        out_ref[g] = sums[...]


def deform(coef_matrix, anchors, nodes):
    rows, points = coef_matrix.shape
    spans = nodes.shape[1]
    width = nodes.shape[2] * nodes.shape[3]
    low = jnp.min(nodes, axis=(2, 3)) - reach
    high = jnp.max(nodes, axis=(2, 3)) + reach
    box_low = jnp.min(low, axis=1)[:, None]
    box_high = jnp.max(high, axis=1)[:, None]
    near = jnp.all((anchors >= box_low) & (anchors <= box_high), axis=0)
    keys = jnp.where(near, anchors[0], 3e38)
    _, order = lax.sort((keys, lax.iota(jnp.int32, points)), num_keys=1, is_stable=False)
    firsts = jnp.sum(keys[None, :] < low[0][:, None], axis=1, dtype=jnp.int32) // BLOCK
    lasts = jnp.sum(keys[None, :] <= high[0][:, None], axis=1, dtype=jnp.int32)
    lasts = (lasts + BLOCK - 1) // BLOCK
    bounds = jnp.stack([firsts, lasts], axis=1).reshape(-1)
    bounds = jnp.concatenate([bounds, jnp.min(firsts)[None], jnp.max(lasts)[None]])
    stacked = jnp.concatenate([coef_matrix, anchors, jnp.zeros((5, points), jnp.float32)], axis=0)
    grouped = nodes.reshape(3, spans, width).transpose(1, 0, 2)
    smem = pl.BlockSpec(memory_space=pltpu.SMEM)
    vmem = pl.BlockSpec(memory_space=pltpu.VMEM)
    shifts = pl.pallas_call(
        deform_kernel,
        out_shape=jax.ShapeDtypeStruct((spans, rows, width), jnp.float32),
        in_specs=[smem, smem, vmem, vmem],
        out_specs=vmem,
        scratch_shapes=[
            pltpu.VMEM((points, BLOCK), jnp.float32),
            pltpu.VMEM((points, BLOCK), jnp.float32),
            pltpu.VMEM((points // BLOCK, 1, 2 * rows, BLOCK), jnp.bfloat16),
            pltpu.VMEM((rows, width), jnp.float32),
        ],
        compiler_params=pltpu.CompilerParams(vmem_limit_bytes=40 << 20),
        name="deform",
    )(order, bounds, stacked, grouped)
    return shifts.transpose(1, 0, 2)


def jacobian_kernel(scales, edges_ref, moved_ref, below_ref, above_ref, left_ref, right_ref, out_ref):
    cells = moved_ref[0]
    spans, chords, normals = cells.shape[1:]
    at_low, at_high, at_left, at_right = [edges_ref[i] == 1 for i in range(4)]
    below = jnp.where(at_low, 2.0 * cells[:, 0] - cells[:, 1], below_ref[0])
    above = jnp.where(at_high, 2.0 * cells[:, spans - 1] - cells[:, spans - 2], above_ref[0])
    chord_pos = lax.broadcasted_iota(jnp.int32, (3, chords, normals), 1)
    normal_pos = lax.broadcasted_iota(jnp.int32, (3, chords, normals), 2)
    for s in range(spans):
        here = cells[:, s]
        before = below if s == 0 else cells[:, s - 1]
        after = above if s == spans - 1 else cells[:, s + 1]
        d_span = (after - before) * scales[0]
        left = jnp.where(at_left, 2.0 * here[:, 0:1] - here[:, 1:2], left_ref[0, :, s : s + 1])
        right = jnp.where(
            at_right,
            2.0 * here[:, chords - 1 :] - here[:, chords - 2 : chords - 1],
            right_ref[0, :, s : s + 1],
        )
        prior = jnp.where(chord_pos == 0, left, pltpu.roll(here, 1, 1))
        later = jnp.where(chord_pos == chords - 1, right, pltpu.roll(here, chords - 1, 1))
        d_chord = (later - prior) * scales[1]
        up = pltpu.roll(here, normals - 1, 2)
        down = pltpu.roll(here, 1, 2)
        inner = jnp.where(normal_pos == 0, 2.0 * here - up, down)
        outer = jnp.where(normal_pos == normals - 1, 2.0 * here - down, up)
        d_normal = (outer - inner) * scales[2]
        out_ref[0, s] = (
            d_span[0] * (d_chord[1] * d_normal[2] - d_chord[2] * d_normal[1])
            + d_span[1] * (d_chord[2] * d_normal[0] - d_chord[0] * d_normal[2])
            + d_span[2] * (d_chord[0] * d_normal[1] - d_chord[1] * d_normal[0])
        )


def shifted(edge, axis, step):
    count = lax.axis_size(axis)
    pairs = [(i, i + step) for i in range(count) if 0 <= i + step < count]
    return lax.ppermute(edge, axis, pairs)


def jacobian_of(moved):
    instances, _, spans, chords, normals = moved.shape
    row_devs, col_devs = lax.axis_size("prow"), lax.axis_size("pcol")
    prow_id, pcol_id = lax.axis_index("prow"), lax.axis_index("pcol")
    below = shifted(moved[:, :, spans - 1], "prow", 1)
    above = shifted(moved[:, :, 0], "prow", -1)
    left = shifted(moved[:, :, :, chords - 1], "pcol", 1)
    right = shifted(moved[:, :, :, 0], "pcol", -1)
    edges = jnp.stack(
        [prow_id == 0, prow_id == row_devs - 1, pcol_id == 0, pcol_id == col_devs - 1]
    ).astype(jnp.int32)
    scales = (spans * row_devs / 2.0, chords * col_devs / 2.0, normals / 2.0)

    def spec(*shape):
        return pl.BlockSpec((1,) + shape, lambda t: (t,) + (0,) * len(shape))

    return pl.pallas_call(
        functools.partial(jacobian_kernel, scales),
        grid=(instances,),
        out_shape=jax.ShapeDtypeStruct((instances, spans, chords, normals), jnp.float32),
        in_specs=[
            pl.BlockSpec(memory_space=pltpu.SMEM),
            spec(3, spans, chords, normals),
            spec(3, chords, normals),
            spec(3, chords, normals),
            spec(3, spans, normals),
            spec(3, spans, normals),
        ],
        out_specs=spec(spans, chords, normals),
        name="jacobian",
    )(edges, moved, below, above, left, right)


def halves(values):
    high = values.astype(jnp.bfloat16)
    return high, (values - high.astype(jnp.float32)).astype(jnp.bfloat16)


def product(values, high, low, dim):
    rows = values.shape[0]
    first, second = halves(values)
    dims = (((1,), (dim,)), ((), ()))
    both = lax.dot_general(
        jnp.concatenate([first, second], axis=0), high, dims, preferred_element_type=jnp.float32
    )
    rest = lax.dot_general(first, low, dims, preferred_element_type=jnp.float32)
    return both[:rows] + both[rows:] + rest


def solve_kernel(
    row_devs, col_devs, block_total, lower_ref, inverse_ref, right_ref, out_ref,
    lower_high, lower_low, inverse_high, inverse_low, forward, solved,
    parts, landed, joined, traded,
    part_send, part_recv, join_send, join_recv, trade_send, trade_recv, out_send, out_recv,
):
    prow_id = lax.axis_index("prow")
    pcol_id = lax.axis_index("pcol")
    pieces = parts.shape[1]
    base = (pcol_id // pieces) * pieces
    piece_id = lax.rem(pcol_id, pieces)
    mesh_ids = pl.DeviceIdType.MESH

    barrier = pltpu.get_barrier_semaphore()
    for o in range(1, col_devs):
        pl.semaphore_signal(
            barrier, 1, device_id={"pcol": lax.rem(pcol_id + o, col_devs)}, device_id_type=mesh_ids
        )
    for o in range(1, row_devs):
        pl.semaphore_signal(
            barrier, 1, device_id={"prow": lax.rem(prow_id + o, row_devs)}, device_id_type=mesh_ids
        )
    for p in range(lower_ref.shape[0]):
        lower_high[p], lower_low[p] = halves(lower_ref[p])
    for k in range(block_total):
        inverse_high[k], inverse_low[k] = halves(inverse_ref[k])
    pl.semaphore_wait(barrier, col_devs + row_devs - 2)

    def pair(i, j):
        return i * (i - 1) // 2 + j

    def sum_pcol(turn, values):
        for q in range(pieces):
            parts[turn, q] = values[:, q * 128 : (q + 1) * 128]
        copies = []
        for o in range(1, col_devs):
            other = lax.rem(pcol_id + o, col_devs)
            copy = pltpu.make_async_remote_copy(
                src_ref=parts.at[turn, lax.rem(other, pieces)],
                dst_ref=landed.at[turn, pcol_id],
                send_sem=part_send.at[o - 1],
                recv_sem=part_recv.at[turn, o - 1],
                device_id={"pcol": other},
                device_id_type=mesh_ids,
            )
            copy.start()
            copies.append(copy)
        landed[turn, pcol_id] = parts[turn, piece_id]
        for copy in copies:
            copy.wait()
        total = landed[turn, 0]
        for d in range(1, col_devs):
            total = total + landed[turn, d]
        joined[turn, piece_id] = total
        copies = []
        for o in range(1, pieces):
            copy = pltpu.make_async_remote_copy(
                src_ref=joined.at[turn, piece_id],
                dst_ref=joined.at[turn, piece_id],
                send_sem=join_send.at[o - 1],
                recv_sem=join_recv.at[turn, o - 1],
                device_id={"pcol": base + lax.rem(piece_id + o, pieces)},
                device_id_type=mesh_ids,
            )
            copy.start()
            copies.append(copy)
        for copy in copies:
            copy.wait()
        return jnp.concatenate([joined[turn, q] for q in range(pieces)], axis=1)

    def sum_prow(turn, values):
        traded[turn, prow_id] = values
        copies = []
        for o in range(1, row_devs):
            copy = pltpu.make_async_remote_copy(
                src_ref=traded.at[turn, prow_id],
                dst_ref=traded.at[turn, prow_id],
                send_sem=trade_send.at[o - 1],
                recv_sem=trade_recv.at[turn, o - 1],
                device_id={"prow": lax.rem(prow_id + o, row_devs)},
                device_id_type=mesh_ids,
            )
            copy.start()
            copies.append(copy)
        for copy in copies:
            copy.wait()
        total = traded[turn, 0]
        for d in range(1, row_devs):
            total = total + traded[turn, d]
        return total

    col_turn = 0
    row_turn = 0
    for k in range(block_total):
        residual = right_ref[k]
        if k > 0:
            partial = None
            for j in range(k):
                term = product(forward[j], lower_high[pair(k, j)], lower_low[pair(k, j)], 1)
                partial = term if partial is None else partial + term
            residual = residual - sum_pcol(col_turn, partial)
            col_turn += 1
        term = product(residual, inverse_high[k], inverse_low[k], 1)
        forward[k] = sum_prow(row_turn, term)
        row_turn += 1
    out_copies = []
    for k in reversed(range(block_total)):
        residual = forward[k]
        if k < block_total - 1:
            partial = None
            for j in range(k + 1, block_total):
                term = product(
                    solved[j, prow_id], lower_high[pair(j, k)], lower_low[pair(j, k)], 0
                )
                partial = term if partial is None else partial + term
            residual = residual - sum_prow(row_turn, partial)
            row_turn += 1
        term = product(residual, inverse_high[k], inverse_low[k], 0)
        solved[k, prow_id] = sum_pcol(col_turn, term)
        col_turn += 1
        for o in range(1, row_devs):
            copy = pltpu.make_async_remote_copy(
                src_ref=solved.at[k, prow_id],
                dst_ref=solved.at[k, prow_id],
                send_sem=out_send.at[k, o - 1],
                recv_sem=out_recv.at[k, o - 1],
                device_id={"prow": lax.rem(prow_id + o, row_devs)},
                device_id_type=mesh_ids,
            )
            copy.start()
            out_copies.append(copy)
    for copy in out_copies:
        copy.wait()
    width = solved.shape[3]
    for k in range(block_total):
        for d in range(row_devs):
            start = (k * row_devs + d) * width
            out_ref[:, start : start + width] = solved[k, d]


def solve(local_factor, local_inverses, right_sides):
    row_devs = lax.axis_size("prow")
    col_devs = lax.axis_size("pcol")
    block_total, row_piece, _, col_piece = local_factor.shape
    row_count = right_sides.shape[0]
    lower = jnp.stack([local_factor[i, :, j] for i in range(block_total) for j in range(i)])
    own = right_sides.reshape(row_count, block_total, row_devs, row_piece)
    own = lax.dynamic_index_in_dim(own, lax.axis_index("prow"), 2, keepdims=False)
    own = own.transpose(1, 0, 2)
    pieces = row_piece // 128
    turns = 2 * block_total - 1
    vmem = pl.BlockSpec(memory_space=pltpu.VMEM)
    dma = pltpu.SemaphoreType.DMA
    narrow = jnp.bfloat16
    wide = jnp.float32
    return pl.pallas_call(
        functools.partial(solve_kernel, row_devs, col_devs, block_total),
        out_shape=jax.ShapeDtypeStruct((row_count, block_total * row_devs * row_piece), wide),
        in_specs=[vmem, vmem, vmem],
        out_specs=vmem,
        scratch_shapes=[
            pltpu.VMEM(lower.shape, narrow),
            pltpu.VMEM(lower.shape, narrow),
            pltpu.VMEM(local_inverses.shape, narrow),
            pltpu.VMEM(local_inverses.shape, narrow),
            pltpu.VMEM((block_total, row_count, col_piece), wide),
            pltpu.VMEM((block_total, row_devs, row_count, row_piece), wide),
            pltpu.VMEM((turns, pieces, row_count, 128), wide),
            pltpu.VMEM((turns, col_devs, row_count, 128), wide),
            pltpu.VMEM((turns, pieces, row_count, 128), wide),
            pltpu.VMEM((turns, row_devs, row_count, col_piece), wide),
            dma((col_devs - 1,)),
            dma((turns, col_devs - 1)),
            dma((pieces - 1,)),
            dma((turns, pieces - 1)),
            dma((row_devs - 1,)),
            dma((turns, row_devs - 1)),
            dma((block_total, row_devs - 1)),
            dma((block_total, row_devs - 1)),
        ],
        compiler_params=pltpu.CompilerParams(
            collective_id=0, has_side_effects=True, vmem_limit_bytes=40 << 20
        ),
        name="solve",
    )(lower, local_inverses, own)


def shards(factor, inverses, targets, anchors, nodes):
    row_devs = lax.axis_size("prow")
    local_factor = factor[:, 0, :, :, 0, :]
    local_inverses = inverses[:, 0, :, 0, :]
    block_total = local_factor.shape[0]
    row_piece = local_factor.shape[1]
    block_len = row_piece * row_devs
    instances = targets.shape[0]
    row_count = instances * targets.shape[1]
    point_total = targets.shape[2]
    right_sides = targets.reshape(row_count, block_total, block_len)
    coef_matrix = solve(local_factor, local_inverses, right_sides)
    shifts = deform(coef_matrix, anchors, nodes).reshape((instances,) + nodes.shape)
    moved = nodes[None] + 2.0 / math.sqrt(point_total) * shifts
    jacobian = jacobian_of(moved)
    return (coef_matrix.reshape(instances, 3, point_total), moved, jacobian)


def solution(mesh):
    placed = (
        P("blade", "prow", None, None, "pcol", None),
        P("blade", "pcol", None, "prow", None),
        P("blade", None, None),
        P("blade", None),
        P("blade", "prow", "pcol", None),
    )
    return jax.shard_map(
        shards,
        mesh=mesh,
        in_specs=placed,
        out_specs=(
            P("blade", None, None),
            P("blade", None, "prow", "pcol", None),
            P("blade", "prow", "pcol", None),
        ),
        check_vma=False,
    )
```

time: 1280 us -> 179 us (0.14)
  matrix products: 827 us -> 0 us
  blocking collectives: 363 us -> 0 us
  Pallas kernels: 0 us -> 124 us
  local copies, waits for them, and re-layouts: 71.1 us -> 22.5 us
    dot_general x32 -> x0, matrix products: 827 us -> none  [the longest x16 806 us: deform(): lax.dot_general(coef_matrix, wendland(dist_sq), (((1,), (1,)), ((), ())),...]
    psum x15 -> x0, blocking collectives: 347 us -> none  [the longest x4 114 us: shards(): summed = lax.psum(partial_value, 'pcol')]
    pallas_call x0 -> x3, Pallas kernels: none -> 124 us  [the longest x1 91 us: solve(): pl.pallas_call(functools.partial(solve_kernel, row_devs, col_devs, block_...]
    slice x40 -> x3, local copies, waits for them, and re-layouts: 37 us -> 0.39 us  [the longest x2 0.35 us: jacobian_of(): above = shifted(moved[:, :, 0], 'prow', -1)]
    squeeze x4 -> x1, local copies, waits for them, and re-layouts: 18.3 us -> 0.65 us  [jacobian_of(): right = shifted(moved[:, :, :, 0], 'pcol', -1)]
    all_gather x1 -> x0, blocking collectives: 16 us -> none  [shards(): coeffs = lax.all_gather(coeffs, 'prow', axis=2, tiled=True)]
  transfers between devices with their start and end apart: 4 -> 4, of which waited for: 3 -> 1; matrix products, arithmetic and copies ran while one was open for 0% -> 2% of each run, Pallas kernels for 0% -> 0%
where the time goes in v1:
time: 179 us; the launch traced here: 176 us
  Pallas kernels  124 us (69%)
  local copies, waits for them, and re-layouts  22.5 us (13%)
  other arithmetic  14.2 us (8%)
  starting transfers between devices  13.5 us (8%)
    pallas_call x1, Pallas kernels, solve(): pl.pallas_call(functools.partial(solve_kernel, row_devs, col_devs, block_...  91 us
    pallas_call x1, Pallas kernels, deform(): pl.pallas_call(deform_kernel, out_shape=jax.ShapeDtypeStruct((spans, rows...  27.5 us
    unnamed x30, local copies, waits for them, and re-layouts  15.2 us
    ppermute x4, starting transfers between devices, shifted(): return lax.ppermute(edge, axis, pairs)  13.5 us
    sort x1, other arithmetic, deform(): lax.sort((keys, lax.iota(jnp.int32, points)), num_keys=1, is_stable=False)  6.8 us
    pallas_call x1, Pallas kernels, jacobian_of(): pl.pallas_call(functools.partial(jacobian_kernel, scales), grid=(instance...  5.59 us
  transfers between devices with their start and end apart: 4, of which 1 were waited for; matrix products, arithmetic and copies ran while one was open for 2% of the time, Pallas kernels for 0%

profile of v1, /device:TPU:1, one launch (start us, length us, event | category | flops | bytes accessed | tf_op | source)
XLA Modules:
  0.0 176.4 jit_solution(17614092249807218526)
XLA Ops:
  0.6 1.0 fusion.10
  1.8 1.1 and_reduce_fusion
  2.9 1.0 reshape_select_fusion
  5.4 1.6 reshape.129
  7.0 0.9 copy.32
  7.9 4.9 %copy.50 = f32[4,1,512,4,1,256]{5,2,3,0,4,1:T(8,128)S(1)} copy(f32[4,1,512,4,1,256]{5,4,3,2,1,0:T(1,128)} %param.5) | data formatting | bytes 16777216 | tf_op args[0]
  13.1 1.7 copy-done
  16.3 1.6 reshape_reshape.3
  17.9 1.3 constant_dynamic-slice_fusion
  19.5 1.0 copy.55
  20.5 6.8 %sort.15 = (f32[8192]{0:T(1024)}, s32[8192]{0:T(1024)S(1)}) sort(f32[8192]{0:T(1024)S(1)} %broadcast_select_fusion, s32[8192]{0:T(1024)S(1)} %iota.3), dimensions={0}, to_apply=%region_5.6 | sort | flops 106496 | bytes 131072 | tf_op jit(solution)/shard_map/sort | solution.py:87
  27.4 1.9 %copy-done.1 = f32[6,512,256]{2,1,0:T(8,128)S(1)} copy-done((f32[6,512,256]{2,1,0:T(8,128)S(1)}, f32[6,512,256]{2,1,0:T(8,128)}, u32[]{:S(2)}) %copy-start.1) | copy-done | bytes 3145752
  29.3 91.0 %solve.1 = f32[24,8192]{1,0:T(8,128)S(1)} custom-call(f32[6,512,256]{2,1,0:T(8,128)S(1)} %copy-done.1, f32[4,256,512]{2,1,0:T(8,128)S(1)} %bitcast.85, f32[4,24,512]{2,1,0:T(8,128)S(1)} %bitcast.86), custom_call_target="tpu_custom_call" | custom-call | tf_op jit(solution)/shard_map/solve/pallas_call | solution.py:358
  120.5 1.3 pad_add_fusion.1.bounds_ref
  121.8 27.5 %deform.1 = f32[4,24,2048]{2,1,0:T(8,128)S(1)} custom-call(s32[8192]{0:T(1024)S(1)} %get-tuple-element.4.order_ref, s32[10]{0:T(128)S(1)} %pad_add_fusion.1.bounds_ref, f32[32,8192]{1,0:T(8,128)S(1)} %maximum_maximum_fusion.stacked_ref, f32[4,3,2048]{2,1,0:T(4,128)S(1)} %bitcast.87), custom_call_target="tpu_custom_call" | custom-call | tf_op jit(solution)/shard_map/deform/pallas_call | solution.py:97
  150.4 2.1 %collective-permute-start = (f32[8,3,16,128]{3,2,1,0:T(8,128)S(1)}, f32[8,3,16,128]{3,2,1,0:T(8,128)S(1)}, u32[]{:S(2)}, u32[]{:S(2)}) collective-permute-start(f32[8,3,16,128]{3,2,1,0:T(8,128)S(1)} %bitcast.96), channel_id=1, source_target_pairs={{0,8},{8,16},{16,24},{1,9},{9,17},{17,25},{2,10},{10,18},{18,26},{... | collective-permute-start | bytes 589832 | tf_op jit(solution)/shard_map/ppermute | solution.py:151
  152.5 2.2 %collective-permute-start.1 = (f32[8,3,16,128]{3,2,1,0:T(8,128)S(1)}, f32[8,3,16,128]{3,2,1,0:T(8,128)S(1)}, u32[]{:S(2)}, u32[]{:S(2)}) collective-permute-start(f32[8,3,16,128]{3,2,1,0:T(8,128)S(1)} %bitcast.97), channel_id=1, source_target_pairs={{8,0},{16,8},{24,16},{9,1},{17,9},{25,17},{10,2},{18,10},{26,18},{... | collective-permute-start | bytes 589832 | tf_op jit(solution)/shard_map/ppermute | solution.py:151
  155.4 7.8 %collective-permute-start.2 = (f32[8,3,4,128]{3,2,1,0:T(4,128)}, f32[8,3,4,128]{3,2,1,0:T(4,128)S(1)}, u32[]{:S(2)}, u32[]{:S(2)}) collective-permute-start(f32[8,3,4,128]{3,2,1,0:T(4,128)} %get-tuple-element.23), channel_id=1, source_target_pairs={{0,1},{1,2},{2,3},{3,4},{4,5},{5,6},{6,7},{8,9},{9,10},{10,11},{11... | collective-permute-start | bytes 147464 | tf_op jit(solution)/shard_map/ppermute | solution.py:151
  163.3 1.3 collective-permute-start.3
  165.5 1.3 copy.40.moved_ref
  166.9 1.3 copy.39
  168.2 1.3 collective-permute-done.3.right_ref
  170.2 0.7 copy-done.6
  170.8 5.6 %jacobian.1 = f32[8,4,16,128]{3,2,1,0:T(8,128)} custom-call(s32[4]{0:T(128)} %add_convert_fusion.edges_ref, f32[8,3,4,16,128]{4,3,2,1,0:T(8,128)} %copy.40.moved_ref, f32[8,3,16,128]{3,2,1,0:T(8,128)} %copy-done.5, f32[8,3,16,128]{3,2,1,0:T(8,128)} %copy-done.6, f32[8,3,4,128]{3,2,1,0:T(4,128)} %copy-done.7, f32[8,3,4,128]{3,2,1,0:T(4,128)} %copy-done.8), custom_call_target="tpu_custom_call" | custom-call | tf_op jit(solution)/shard_map/jacobian/pallas_call | solution.py:170
  (52 shorter events, 7.3 us)
Async XLA Ops:
  12.8 2.4 %copy-start.2 = (f32[4,1,256,1,512]{4,3,2,1,0:T(1,128)S(1)}, f32[4,1,256,1,512]{4,3,2,1,0:T(1,128)}, u32[]{:S(2)}) copy-start(f32[4,1,256,1,512]{4,3,2,1,0:T(1,128)} %param.6) | copy-start | bytes 6291460
  13.0 2.7 %copy-start.3 = (f32[8,3,8192]{2,0,1:T(8,128)S(1)}, f32[8,3,8192]{2,0,1:T(8,128)}, u32[]{:S(2)}) copy-start(f32[8,3,8192]{2,0,1:T(8,128)} %param.7) | copy-start | bytes 2359300
  13.1 1.7 copy-start
  19.5 100.8 %copy-start.4 = (f32[3,8192]{1,0:T(4,128)S(1)}, f32[3,8192]{1,0:T(4,128)}, u32[]{:S(2)}) copy-start(f32[3,8192]{1,0:T(4,128)} %param.8) | copy-start | bytes 294916
  27.4 1.9 %copy-start.1 = (f32[6,512,256]{2,1,0:T(8,128)S(1)}, f32[6,512,256]{2,1,0:T(8,128)}, u32[]{:S(2)}) copy-start(f32[6,512,256]{2,1,0:T(8,128)} %copy-done) | copy-start | bytes 9437188
  150.4 19.1 %collective-permute-start = (f32[8,3,16,128]{3,2,1,0:T(8,128)S(1)}, f32[8,3,16,128]{3,2,1,0:T(8,128)S(1)}, u32[]{:S(2)}, u32[]{:S(2)}) collective-permute-start(f32[8,3,16,128]{3,2,1,0:T(8,128)S(1)} %bitcast.96), channel_id=1, source_target_pairs={{0,8},{8,16},{16,24},{1,9},{9,17},{17,25},{2,10},{10,18},{18,26},{... | collective-permute-start | bytes 589832 | tf_op jit(solution)/shard_map/ppermute | solution.py:151
  152.5 16.9 %collective-permute-start.1 = (f32[8,3,16,128]{3,2,1,0:T(8,128)S(1)}, f32[8,3,16,128]{3,2,1,0:T(8,128)S(1)}, u32[]{:S(2)}, u32[]{:S(2)}) collective-permute-start(f32[8,3,16,128]{3,2,1,0:T(8,128)S(1)} %bitcast.97), channel_id=1, source_target_pairs={{8,0},{16,8},{24,16},{9,1},{17,9},{25,17},{10,2},{18,10},{26,18},{... | collective-permute-start | bytes 589832 | tf_op jit(solution)/shard_map/ppermute | solution.py:151
  155.4 12.8 %collective-permute-start.2 = (f32[8,3,4,128]{3,2,1,0:T(4,128)}, f32[8,3,4,128]{3,2,1,0:T(4,128)S(1)}, u32[]{:S(2)}, u32[]{:S(2)}) collective-permute-start(f32[8,3,4,128]{3,2,1,0:T(4,128)} %get-tuple-element.23), channel_id=1, source_target_pairs={{0,1},{1,2},{2,3},{3,4},{4,5},{5,6},{6,7},{8,9},{9,10},{10,11},{11... | collective-permute-start | bytes 147464 | tf_op jit(solution)/shard_map/ppermute | solution.py:151
  163.3 6.2 %collective-permute-start.3 = (f32[8,3,4,128]{3,2,1,0:T(4,128)}, f32[8,3,4,128]{3,2,1,0:T(4,128)S(1)}, u32[]{:S(2)}, u32[]{:S(2)}) collective-permute-start(f32[8,3,4,128]{3,2,1,0:T(4,128)} %get-tuple-element.22), channel_id=1, source_target_pairs={{1,0},{2,1},{3,2},{4,3},{5,4},{6,5},{7,6},{9,8},{10,9},{11,10},{12... | collective-permute-start | bytes 147464 | tf_op jit(solution)/shard_map/ppermute | solution.py:151
  168.2 1.3 copy-start.7
  169.5 0.6 copy-start.8
  169.5 0.7 copy-start.5
  170.2 0.7 copy-start.6

commit v2 on v1

--- a/solution.py
+++ b/solution.py
@@ -111,77 +111,124 @@
     return shifts.transpose(1, 0, 2)
 
 
-def jacobian_kernel(scales, edges_ref, moved_ref, below_ref, above_ref, left_ref, right_ref, out_ref):
-    cells = moved_ref[0]
-    spans, chords, normals = cells.shape[1:]
-    at_low, at_high, at_left, at_right = [edges_ref[i] == 1 for i in range(4)]
-    below = jnp.where(at_low, 2.0 * cells[:, 0] - cells[:, 1], below_ref[0])
-    above = jnp.where(at_high, 2.0 * cells[:, spans - 1] - cells[:, spans - 2], above_ref[0])
+def jacobian_kernel(
+    scales, row_devs, col_devs, moved_ref, out_ref,
+    first, last, below, above, left, right, send, recv,
+):
+    instances, _, spans, chords, normals = moved_ref.shape
+    prow_id = lax.axis_index("prow")
+    pcol_id = lax.axis_index("pcol")
+    mesh_ids = pl.DeviceIdType.MESH
+    barrier = pltpu.get_barrier_semaphore()
+    for axis, place, count in (("prow", prow_id, row_devs), ("pcol", pcol_id, col_devs)):
+        for step in (1, count - 1):
+            pl.semaphore_signal(
+                barrier, 1, device_id={axis: lax.rem(place + step, count)}, device_id_type=mesh_ids
+            )
+    first[...] = moved_ref[:, :, :, 0:1, :]
+    last[...] = moved_ref[:, :, :, chords - 1 : chords, :]
+    pl.semaphore_wait(barrier, 4)
+
+    def transfer(n, source, target, axis, place):
+        return pltpu.make_async_remote_copy(
+            src_ref=source,
+            dst_ref=target,
+            send_sem=send.at[n],
+            recv_sem=recv.at[n],
+            device_id={axis: place},
+            device_id_type=mesh_ids,
+        )
+
+    upward = transfer(
+        0, moved_ref.at[:, :, spans - 1], below, "prow", lax.rem(prow_id + 1, row_devs)
+    )
+    downward = transfer(
+        1, moved_ref.at[:, :, 0], above, "prow", lax.rem(prow_id + row_devs - 1, row_devs)
+    )
+    onward = transfer(2, last, left, "pcol", lax.rem(pcol_id + 1, col_devs))
+    backward = transfer(3, first, right, "pcol", lax.rem(pcol_id + col_devs - 1, col_devs))
+    at_low, at_high = prow_id == 0, prow_id == row_devs - 1
+    at_left, at_right = pcol_id == 0, pcol_id == col_devs - 1
+    plans = (
+        (upward, at_high, at_low),
+        (downward, at_low, at_high),
+        (onward, at_right, at_left),
+        (backward, at_left, at_right),
+    )
+    for copy, closed, _ in plans:
+        pl.when(jnp.logical_not(closed))(copy.start)
+
+    @pl.when(at_low)
+    def _():
+        below[...] = 2.0 * moved_ref[:, :, 0] - moved_ref[:, :, 1]
+
+    @pl.when(at_high)
+    def _():
+        above[...] = 2.0 * moved_ref[:, :, spans - 1] - moved_ref[:, :, spans - 2]
+
+    @pl.when(at_left)
+    def _():
+        left[...] = 2.0 * moved_ref[:, :, :, 0:1, :] - moved_ref[:, :, :, 1:2, :]
+
+    @pl.when(at_right)
+    def _():
+        right[...] = (
+            2.0 * moved_ref[:, :, :, chords - 1 : chords, :]
+            - moved_ref[:, :, :, chords - 2 : chords - 1, :]
+        )
+
+    for copy, closed, edge in plans:
+        pl.when(jnp.logical_not(closed))(copy.wait_send)
+        pl.when(jnp.logical_not(edge))(copy.wait_recv)
+
     chord_pos = lax.broadcasted_iota(jnp.int32, (3, chords, normals), 1)
     normal_pos = lax.broadcasted_iota(jnp.int32, (3, chords, normals), 2)
-    for s in range(spans):
-        here = cells[:, s]
-        before = below if s == 0 else cells[:, s - 1]
-        after = above if s == spans - 1 else cells[:, s + 1]
-        d_span = (after - before) * scales[0]
-        left = jnp.where(at_left, 2.0 * here[:, 0:1] - here[:, 1:2], left_ref[0, :, s : s + 1])
-        right = jnp.where(
-            at_right,
-            2.0 * here[:, chords - 1 :] - here[:, chords - 2 : chords - 1],
-            right_ref[0, :, s : s + 1],
-        )
-        prior = jnp.where(chord_pos == 0, left, pltpu.roll(here, 1, 1))
-        later = jnp.where(chord_pos == chords - 1, right, pltpu.roll(here, chords - 1, 1))
-        d_chord = (later - prior) * scales[1]
-        up = pltpu.roll(here, normals - 1, 2)
-        down = pltpu.roll(here, 1, 2)
-        inner = jnp.where(normal_pos == 0, 2.0 * here - up, down)
-        outer = jnp.where(normal_pos == normals - 1, 2.0 * here - down, up)
-        d_normal = (outer - inner) * scales[2]
-        out_ref[0, s] = (
-            d_span[0] * (d_chord[1] * d_normal[2] - d_chord[2] * d_normal[1])
-            + d_span[1] * (d_chord[2] * d_normal[0] - d_chord[0] * d_normal[2])
-            + d_span[2] * (d_chord[0] * d_normal[1] - d_chord[1] * d_normal[0])
-        )
-
-
-def shifted(edge, axis, step):
-    count = lax.axis_size(axis)
-    pairs = [(i, i + step) for i in range(count) if 0 <= i + step < count]
-    return lax.ppermute(edge, axis, pairs)
+
+    @pl.loop(0, instances)
+    def _(t):
+        for s in range(spans):
+            here = moved_ref[t, :, s]
+            before = below[t] if s == 0 else moved_ref[t, :, s - 1]
+            after = above[t] if s == spans - 1 else moved_ref[t, :, s + 1]
+            d_span = (after - before) * scales[0]
+            prior = jnp.where(chord_pos == 0, left[t, :, s], pltpu.roll(here, 1, 1))
+            later = jnp.where(
+                chord_pos == chords - 1, right[t, :, s], pltpu.roll(here, chords - 1, 1)
+            )
+            d_chord = (later - prior) * scales[1]
+            up = pltpu.roll(here, normals - 1, 2)
+            down = pltpu.roll(here, 1, 2)
+            inner = jnp.where(normal_pos == 0, 2.0 * here - up, down)
+            outer = jnp.where(normal_pos == normals - 1, 2.0 * here - down, up)
+            d_normal = (outer - inner) * scales[2]
+            out_ref[t, s] = (
+                d_span[0] * (d_chord[1] * d_normal[2] - d_chord[2] * d_normal[1])
+                + d_span[1] * (d_chord[2] * d_normal[0] - d_chord[0] * d_normal[2])
+                + d_span[2] * (d_chord[0] * d_normal[1] - d_chord[1] * d_normal[0])
+            )
 
 
 def jacobian_of(moved):
     instances, _, spans, chords, normals = moved.shape
     row_devs, col_devs = lax.axis_size("prow"), lax.axis_size("pcol")
-    prow_id, pcol_id = lax.axis_index("prow"), lax.axis_index("pcol")
-    below = shifted(moved[:, :, spans - 1], "prow", 1)
-    above = shifted(moved[:, :, 0], "prow", -1)
-    left = shifted(moved[:, :, :, chords - 1], "pcol", 1)
-    right = shifted(moved[:, :, :, 0], "pcol", -1)
-    edges = jnp.stack(
-        [prow_id == 0, prow_id == row_devs - 1, pcol_id == 0, pcol_id == col_devs - 1]
-    ).astype(jnp.int32)
     scales = (spans * row_devs / 2.0, chords * col_devs / 2.0, normals / 2.0)
-
-    def spec(*shape):
-        return pl.BlockSpec((1,) + shape, lambda t: (t,) + (0,) * len(shape))
-
+    vmem = pl.BlockSpec(memory_space=pltpu.VMEM)
+    layer = pltpu.VMEM((instances, 3, chords, normals), jnp.float32)
+    column = pltpu.VMEM((instances, 3, spans, 1, normals), jnp.float32)
     return pl.pallas_call(
-        functools.partial(jacobian_kernel, scales),
-        grid=(instances,),
+        functools.partial(jacobian_kernel, scales, row_devs, col_devs),
         out_shape=jax.ShapeDtypeStruct((instances, spans, chords, normals), jnp.float32),
-        in_specs=[
-            pl.BlockSpec(memory_space=pltpu.SMEM),
-            spec(3, spans, chords, normals),
-            spec(3, chords, normals),
-            spec(3, chords, normals),
-            spec(3, spans, normals),
-            spec(3, spans, normals),
+        in_specs=[vmem],
+        out_specs=vmem,
+        scratch_shapes=[
+            column, column, layer, layer, column, column,
+            pltpu.SemaphoreType.DMA((4,)), pltpu.SemaphoreType.DMA((4,)),
         ],
-        out_specs=spec(spans, chords, normals),
+        compiler_params=pltpu.CompilerParams(
+            collective_id=1, has_side_effects=True, vmem_limit_bytes=32 << 20
+        ),
         name="jacobian",
-    )(edges, moved, below, above, left, right)
+    )(moved)
 
 
 def halves(values):
@@ -231,7 +278,7 @@
     def pair(i, j):
         return i * (i - 1) // 2 + j
 
-    def sum_pcol(turn, values):
+    def sum_pcol(turn, values, meanwhile=None):
         for q in range(pieces):
             parts[turn, q] = values[:, q * 128 : (q + 1) * 128]
         copies = []
@@ -248,6 +295,7 @@
             copy.start()
             copies.append(copy)
         landed[turn, pcol_id] = parts[turn, piece_id]
+        extra = None if meanwhile is None else meanwhile()
         for copy in copies:
             copy.wait()
         total = landed[turn, 0]
@@ -268,9 +316,9 @@
             copies.append(copy)
         for copy in copies:
             copy.wait()
-        return jnp.concatenate([joined[turn, q] for q in range(pieces)], axis=1)
-
-    def sum_prow(turn, values):
+        return jnp.concatenate([joined[turn, q] for q in range(pieces)], axis=1), extra
+
+    def sum_prow(turn, values, meanwhile=None):
         traded[turn, prow_id] = values
         copies = []
         for o in range(1, row_devs):
@@ -284,41 +332,55 @@
             )
             copy.start()
             copies.append(copy)
+        extra = None if meanwhile is None else meanwhile()
         for copy in copies:
             copy.wait()
         total = traded[turn, 0]
         for d in range(1, row_devs):
             total = total + traded[turn, d]
-        return total
+        return total, extra
+
+    def behind(k, known):
+        partial = None
+        for j in known:
+            term = product(forward[j], lower_high[pair(k, j)], lower_low[pair(k, j)], 1)
+            partial = term if partial is None else partial + term
+        return partial
+
+    def ahead(k, known):
+        partial = None
+        for j in known:
+            term = product(solved[j, prow_id], lower_high[pair(j, k)], lower_low[pair(j, k)], 0)
+            partial = term if partial is None else partial + term
+        return partial
+
+    def joint(early, late):
+        return late if early is None else early + late
 
     col_turn = 0
     row_turn = 0
     for k in range(block_total):
         residual = right_ref[k]
         if k > 0:
-            partial = None
-            for j in range(k):
-                term = product(forward[j], lower_high[pair(k, j)], lower_low[pair(k, j)], 1)
-                partial = term if partial is None else partial + term
-            residual = residual - sum_pcol(col_turn, partial)
+            partial = joint(early, behind(k, [k - 1]))
+            summed, _ = sum_pcol(col_turn, partial)
+            residual = residual - summed
             col_turn += 1
         term = product(residual, inverse_high[k], inverse_low[k], 1)
-        forward[k] = sum_prow(row_turn, term)
+        later = functools.partial(behind, k + 1, range(k)) if k + 1 < block_total else None
+        forward[k], early = sum_prow(row_turn, term, later)
         row_turn += 1
     out_copies = []
     for k in reversed(range(block_total)):
         residual = forward[k]
         if k < block_total - 1:
-            partial = None
-            for j in range(k + 1, block_total):
-                term = product(
-                    solved[j, prow_id], lower_high[pair(j, k)], lower_low[pair(j, k)], 0
-                )
-                partial = term if partial is None else partial + term
-            residual = residual - sum_prow(row_turn, partial)
+            partial = joint(early, ahead(k, [k + 1]))
+            summed, _ = sum_prow(row_turn, partial)
+            residual = residual - summed
             row_turn += 1
         term = product(residual, inverse_high[k], inverse_low[k], 0)
-        solved[k, prow_id] = sum_pcol(col_turn, term)
+        later = functools.partial(ahead, k - 1, range(k + 1, block_total)) if k > 0 else None
+        solved[k, prow_id], early = sum_pcol(col_turn, term, later)
         col_turn += 1
         for o in range(1, row_devs):
             copy = pltpu.make_async_remote_copy(

time: 179 us -> 158 us (0.88); the launches traced: 176 us -> 158 us
  starting transfers between devices: 13.5 us -> 0 us
  local copies, waits for them, and re-layouts: 22.5 us -> 16 us
  Pallas kernels: 124 us -> 130 us
  other arithmetic: 14.2 us -> 10.8 us
    ppermute x4 -> x0, starting transfers between devices: 13.5 us -> none  [shifted(): return lax.ppermute(edge, axis, pairs)]
    pallas_call x1, Pallas kernels: 5.59 us -> 13.4 us  [jacobian_of(): pl.pallas_call(functools.partial(jacobian_kernel, scales, row_devs, col_d...]
    unnamed x30 -> x25, local copies, waits for them, and re-layouts: 15.2 us -> 12.3 us
    reshape x2, local copies, waits for them, and re-layouts: 2.56 us -> 0.11 us  [deform(): grouped = nodes.reshape(3, spans, width).transpose(1, 0, 2)]
  transfers between devices with their start and end apart: 4 -> 0, of which waited for: 1 -> 0; matrix products, arithmetic and copies ran while one was open for 2% -> 0% of each run, Pallas kernels for 0% -> 0%
where the time goes in v2:
time: 158 us
  Pallas kernels  130 us (82%)
  local copies, waits for them, and re-layouts  16 us (10%)
  other arithmetic  10.8 us (7%)
    pallas_call x1, Pallas kernels, solve(): pl.pallas_call(functools.partial(solve_kernel, row_devs, col_devs, block_...  90.6 us
    pallas_call x1, Pallas kernels, deform(): pl.pallas_call(deform_kernel, out_shape=jax.ShapeDtypeStruct((spans, rows...  26.5 us
    pallas_call x1, Pallas kernels, jacobian_of(): pl.pallas_call(functools.partial(jacobian_kernel, scales, row_devs, col_d...  13.4 us
    unnamed x25, local copies, waits for them, and re-layouts  12.3 us
    sort x1, other arithmetic, deform(): lax.sort((keys, lax.iota(jnp.int32, points)), num_keys=1, is_stable=False)  6.98 us

profile of v2, /device:TPU:1, one launch (start us, length us, event | category | flops | bytes accessed | tf_op | source)
XLA Modules:
  0.0 158.2 jit_solution(13277831852285363228)
XLA Ops:
  0.6 4.9 %copy.35 = f32[4,1,512,4,1,256]{5,2,3,0,4,1:T(8,128)S(1)} copy(f32[4,1,512,4,1,256]{5,4,3,2,1,0:T(1,128)} %param.5) | data formatting | bytes 16777216 | tf_op args[0]
  5.8 1.7 %copy-done = f32[6,512,256]{2,1,0:T(8,128)} copy-done((f32[6,512,256]{2,1,0:T(8,128)}, f32[6,512,256]{2,1,0:T(8,128)S(1)}, u32[]{:S(2)}) %copy-start) | copy-done | bytes 3145752
  7.5 0.4 copy-done.3
  7.9 0.2 copy.36
  8.1 0.3 copy-done.5
  8.4 0.5 copy.21
  9.0 1.6 %reshape_reshape.3 = f32[24,4,4,512]{3,2,1,0:T(4,128)} reshape(f32[8,3,8192]{2,1,0:T(4,128)S(1)} %copy.21) | data formatting | bytes 1572864 | tf_op jit(solution)/shard_map/reshape;reshape | solution.py:411
  10.6 1.3 constant_dynamic-slice_fusion
  12.0 1.9 %copy-done.1 = f32[6,512,256]{2,1,0:T(8,128)S(1)} copy-done((f32[6,512,256]{2,1,0:T(8,128)S(1)}, f32[6,512,256]{2,1,0:T(8,128)}, u32[]{:S(2)}) %copy-start.1) | copy-done | bytes 3145752
  13.9 90.6 %solve.1 = f32[24,8192]{1,0:T(8,128)S(1)} custom-call(f32[6,512,256]{2,1,0:T(8,128)S(1)} %copy-done.1, f32[4,256,512]{2,1,0:T(8,128)S(1)} %bitcast.71, f32[4,24,512]{2,1,0:T(8,128)S(1)} %bitcast.72), custom_call_target="tpu_custom_call" | custom-call | tf_op jit(solution)/shard_map/solve/pallas_call | solution.py:420
  104.5 0.3 reshape.127
  104.9 1.3 copy.26
  106.3 0.1 broadcast_add_fusion
  106.5 0.2 and_reduce_fusion
  106.8 7.0 %sort.15 = (f32[8192]{0:T(1024)}, s32[8192]{0:T(1024)S(1)}) sort(f32[8192]{0:T(1024)S(1)} %broadcast_select_fusion, s32[8192]{0:T(1024)S(1)} %iota.3), dimensions={0}, to_apply=%region_5.6 | sort | flops 106496 | bytes 131072 | tf_op jit(solution)/shard_map/sort | solution.py:87
  113.8 0.3 convert_reduce_fusion.1
  114.0 0.6 fusion.6
  114.7 0.6 fusion.7
  115.5 1.4 pad_add_fusion.1.bounds_ref
  117.0 0.1 maximum_maximum_fusion.stacked_ref
  117.3 26.5 %deform.1 = f32[4,24,2048]{2,1,0:T(8,128)S(1)} custom-call(s32[8192]{0:T(1024)S(1)} %get-tuple-element.4.order_ref, s32[10]{0:T(128)S(1)} %pad_add_fusion.1.bounds_ref, f32[32,8192]{1,0:T(8,128)S(1)} %maximum_maximum_fusion.stacked_ref, f32[4,3,2048]{2,1,0:T(4,128)S(1)} %bitcast.73), custom_call_target="tpu_custom_call" | custom-call | tf_op jit(solution)/shard_map/deform/pallas_call | solution.py:97
  143.8 0.1 copy.29
  144.1 13.4 %jacobian.1 = f32[8,4,16,128]{3,2,1,0:T(8,128)S(1)} custom-call(f32[8,3,4,16,128]{4,3,2,1,0:T(8,128)S(1)} %copy_add_fusion.moved_ref), custom_call_target="tpu_custom_call" | custom-call | tf_op jit(solution)/shard_map/jacobian/pallas_call | solution.py:218
  157.5 0.7 copy.45
  (34 shorter events, 1.1 us)
Async XLA Ops:
  5.5 2.4 %copy-start.3 = (f32[4,1,256,1,512]{4,3,2,1,0:T(1,128)S(1)}, f32[4,1,256,1,512]{4,3,2,1,0:T(1,128)}, u32[]{:S(2)}) copy-start(f32[4,1,256,1,512]{4,3,2,1,0:T(1,128)} %param.6) | copy-start | bytes 6291460
  5.7 2.7 %copy-start.5 = (f32[8,3,8192]{2,0,1:T(8,128)S(1)}, f32[8,3,8192]{2,0,1:T(8,128)}, u32[]{:S(2)}) copy-start(f32[8,3,8192]{2,0,1:T(8,128)} %param.7) | copy-start | bytes 2359300
  5.8 1.7 %copy-start = (f32[6,512,256]{2,1,0:T(8,128)}, f32[6,512,256]{2,1,0:T(8,128)S(1)}, u32[]{:S(2)}) copy-start(f32[6,512,256]{2,1,0:T(8,128)S(1)} %fusion.lower_ref) | copy-start | bytes 9437188
  12.0 1.9 %copy-start.1 = (f32[6,512,256]{2,1,0:T(8,128)S(1)}, f32[6,512,256]{2,1,0:T(8,128)}, u32[]{:S(2)}) copy-start(f32[6,512,256]{2,1,0:T(8,128)} %copy-done) | copy-start | bytes 9437188
  104.5 1.7 %copy-start.4 = (f32[3,4,16,128]{3,2,1,0:T(8,128)S(1)}, f32[3,4,16,128]{3,2,1,0:T(8,128)}, u32[]{:S(2)}) copy-start(f32[3,4,16,128]{3,2,1,0:T(8,128)} %param.9) | copy-start | bytes 294916
  104.5 2.0 %copy-start.6 = (f32[3,8192]{1,0:T(4,128)S(1)}, f32[3,8192]{1,0:T(4,128)}, u32[]{:S(2)}) copy-start(f32[3,8192]{1,0:T(4,128)} %param.8) | copy-start | bytes 294916
  144.1 14.1 %copy-start.2 = (f32[8,3,4,16,128]{4,3,2,1,0:T(8,128)}, f32[8,3,4,16,128]{4,3,2,1,0:T(8,128)S(1)}, u32[]{:S(2)}) copy-start(f32[8,3,4,16,128]{4,3,2,1,0:T(8,128)S(1)} %copy_add_fusion.moved_ref) | copy-start | bytes 2359300
